TPU v7x, 32 devices: a whole 2x2x4 slice. The times are simulated.
32 devices in a mesh: feat: 8 (over z, y), ex: 4 (over x, core).
Axes of the slice: x: 2, y: 2, z: 4, core: 2. Of those that a mesh axis runs over, the one named last changes fastest.
Arguments:
- examples: bfloat16 [4096, 262144], P('ex', 'feat'), may hold values from -6 to 6
- weights: bfloat16 [262144], P('feat'), may hold values from -0.01171875 to 0.01171875
- labels: int32 [4096], P('ex'), may hold values from 0 to 1
- split: int32 [4096], P('ex'), may hold values 0 or 1
- val_weight: float32 [32, 4096], P(None, 'ex'), may hold values from 0.1 to 10
- strengths: float32 [256], replicated, may hold values from 0.05 to 1
- block_ids: int32 [262144], P('feat'), may hold values from 0 to 255
Outputs:
- solve: float32 [32, 262144], P(None, ('feat', 'ex'))
- hypergrad: float32 [32, 256], P(None, ('feat', 'ex'))
All inputs are finite; a program needn't handle non-finite values. No bound on the sum of `split` on one device may be relied on, other than what follows from the above.
Results may differ from a plain program's by a relative error of at most 0.0029.
Values may be sent and summed in bfloat16 or wider, within the bound.
A program may use at most 128 MiB of HBM per device.

v0:
```python
import jax
import jax.numpy as jnp
from jax import lax
from jax.sharding import PartitionSpec as P


def shards(examples, weights, labels, split, val_weight, strengths, block_ids):
    n_ex = lax.axis_size("ex")
    n_feat = lax.axis_size("feat")
    ex_pos = lax.axis_index("ex")
    feat_pos = lax.axis_index("feat")
    total = examples.shape[0] * n_ex
    width = examples.shape[1]
    share = width // n_ex
    blocks = strengths.shape[0]
    nb_local = blocks // (n_feat * n_ex)
    margin = lax.psum(jnp.dot(examples, weights, preferred_element_type=jnp.float32), "feat")
    prob = 1.0 / (1.0 + jnp.exp(-margin))
    train = split.astype(jnp.float32)
    curvew = train * prob * (1.0 - prob)
    err = (1.0 - train) * (prob - labels.astype(jnp.float32))
    gradw = (val_weight * err[None, :] / jnp.sqrt(jnp.float32(total))).astype(jnp.bfloat16)
    grad_part = jnp.dot(gradw, examples, preferred_element_type=jnp.float32)
    onehot = (block_ids[:, None] == jnp.arange(blocks, dtype=jnp.int32)[None, :]).astype(
        jnp.float32
    )
    lamf = jnp.dot(onehot, strengths, precision=lax.Precision.HIGHEST)
    wfloat = weights.astype(jnp.float32)
    start = ex_pos * share
    rhs = lax.psum_scatter(grad_part, "ex", scatter_dimension=1, tiled=True)
    lam_loc = lax.dynamic_slice_in_dim(lamf, start, share, 0)
    onehot_loc = lax.dynamic_slice_in_dim(onehot, start, share, 0)
    w_loc = lax.dynamic_slice_in_dim(wfloat, start, share, 0)

    def norm_sum(vec):
        return lax.psum(jnp.sum(vec * vec, axis=1), ("feat", "ex"))

    solve = jnp.zeros_like(rhs)
    resid = rhs
    direc = rhs
    norm_now = norm_sum(resid)
    for step in range(2):
        full_dir = lax.all_gather(direc.astype(jnp.bfloat16), "ex", axis=1, tiled=True)
        tang = lax.dot_general(
            full_dir, examples, (((1,), (1,)), ((), ())), preferred_element_type=jnp.float32
        )
        tang = lax.psum(tang, "feat")
        wtang = (curvew[None, :] * tang).astype(jnp.bfloat16)
        prod = lax.psum_scatter(
            jnp.dot(wtang, examples, preferred_element_type=jnp.float32),
            "ex",
            scatter_dimension=1,
            tiled=True,
        )
        image = prod / jnp.float32(total) + lam_loc[None, :] * direc
        alpha = norm_now / lax.psum(jnp.sum(direc * image, axis=1), ("feat", "ex"))
        solve = solve + alpha[:, None] * direc
        resid = resid - alpha[:, None] * image
        if step == 0:
            norm_next = norm_sum(resid)
            direc = resid + (norm_next / norm_now)[:, None] * direc
            norm_now = norm_next
    partial_blocks = jnp.dot(solve * w_loc[None, :], onehot_loc, precision=lax.Precision.HIGHEST)
    block_sums = lax.psum_scatter(partial_blocks, ("feat", "ex"), scatter_dimension=1, tiled=True)
    own = lax.dynamic_slice_in_dim(strengths, (feat_pos * n_ex + ex_pos) * nb_local, nb_local, 0)
    return (solve, -own[None, :] * block_sums)


def solution(mesh):
    placed = (P("ex", "feat"), P("feat"), P("ex"), P("ex"), P(None, "ex"), P(), P("feat"))
    return jax.shard_map(
        shards,
        mesh=mesh,
        in_specs=placed,
        out_specs=(P(None, ("feat", "ex")), P(None, ("feat", "ex"))),
        check_vma=False,
    )
```

profile of v0, /device:TPU:0, one launch (start us, length us, event | category | flops | bytes accessed | tf_op | source)
XLA Modules:
  0.0 695.1 jit_solution(9688805539957404620)
XLA Ops:
  7.2 0.9 reshape.14
  8.2 26.6 %fusion.15 = f32[1,1024]{1,0:T(1,128)S(1)} fusion(bf16[1024,32768]{1,0:T(8,128)(2,1)} %param.7, bf16[32768,1]{0,1:T(2,128)(2,1)S(1)} %reshape.14), kind=kOutput, calls=%fused_computation.33 | convolution fusion | flops 67108864 | bytes 67178496 | tf_op jit(solution)/shard_map/dot_general | solution.py:17
  34.8 23.2 %psum.49 = f32[1024]{0:T(1024)S(1)} all-reduce(f32[1024]{0:T(1024)S(1)} %bitcast.13), channel_id=1, replica_groups=mesh['feat'=8,'ex'=4] {'feat'}, use_global_device_ids=true, to_apply=%region_0.0 | all-reduce | flops 1024 | bytes 8192 | tf_op jit(solution)/shard_map/psum | solution.py:17
  58.0 25.3 %fusion.5 = f32[32,32768]{1,0:T(8,128)} fusion(bf16[1024,32768]{1,0:T(8,128)(2,1)} %param.7, f32[32,1024]{1,0:T(8,128)S(1)} %copy-done.3, f32[1024]{0:T(1024)S(1)} %get-tuple-element.7), kind=kOutput, calls=%fused_computation.17 | convolution fusion | flops 2147581952 | bytes 71438336 | tf_op jit(solution)/shard_map/dot_general | solution.py:23
  83.3 41.8 %reduce-scatter.4.cloned.1.call-done = f32[32,8192]{1,0:T(8,128)} async-done(((f32[32,32768]{1,0:T(8,128)}), f32[32,8192]{1,0:T(8,128)}) %reduce-scatter.4.cloned.1.call-update) | async-done | bytes 1048592 | tf_op jit(solution)/shard_map/reduce_scatter | solution.py:30
  125.2 2.1 convert_element_type.28
  127.2 0.0 all-reduce.5.cloned.1.call-start
  127.3 22.7 %all-gather.3.cloned.1.call-done = bf16[32,32768]{1,0:T(8,128)(2,1)} async-done(((bf16[32,8192]{1,0:T(8,128)(2,1)}), bf16[32,32768]{1,0:T(8,128)(2,1)}) %all-gather.3.cloned.1.call-update) | async-done | bytes 2097168 | tf_op jit(solution)/shard_map/all_gather | solution.py:43
  150.0 27.6 %fusion.16 = f32[32,1024]{1,0:T(8,128)} fusion(bf16[32,32768]{1,0:T(8,128)(2,1)} %all-gather.3.cloned.1.call-done, bf16[1024,32768]{1,0:T(8,128)(2,1)} %param.7), kind=kOutput, calls=%fused_computation.34 | convolution fusion | flops 2147483648 | bytes 69337088 | tf_op jit(solution)/shard_map/dot_general | solution.py:44
  177.7 70.5 %all-reduce.5.cloned.1.call-done = f32[32,1024]{1,0:T(8,128)} async-done(((f32[32,1024]{1,0:T(8,128)}), f32[32,1024]{1,0:T(8,128)}) %all-reduce.5.cloned.1.call-update) | async-done | bytes 131088 | tf_op jit(solution)/shard_map/psum | solution.py:47
  248.2 26.5 %fusion.6 = f32[32,32768]{1,0:T(8,128)} fusion(bf16[1024,32768]{1,0:T(8,128)(2,1)} %param.7, f32[32,1024]{1,0:T(8,128)} %all-reduce.5.cloned.1.call-done, f32[1024]{0:T(1024)S(1)} %get-tuple-element.6), kind=kOutput, calls=%fused_computation.18 | convolution fusion | flops 2147549184 | bytes 71438336 | tf_op jit(solution)/shard_map/dot_general | solution.py:50
  274.7 17.1 %fusion.3 = f32[1,32768]{1,0:T(1,128)S(1)} fusion(f32[256,1]{0,1:T(1,128)S(1)} %bitcast.15, s32[32768]{0:T(1024)S(1)} %copy-done.4), kind=kOutput, calls=%fused_computation.12 | convolution fusion | flops 109051904 | bytes 263168 | tf_op jit(solution)/shard_map/dot_general | solution.py:27
  291.8 26.6 %reduce-scatter.6.cloned.1.call-done = f32[32,8192]{1,0:T(8,128)} async-done(((f32[32,32768]{1,0:T(8,128)}), f32[32,8192]{1,0:T(8,128)}) %reduce-scatter.6.cloned.1.call-update) | async-done | bytes 1048592 | tf_op jit(solution)/shard_map/reduce_scatter | solution.py:49
  318.4 1.6 multiply_reduce_fusion.2
  320.0 39.3 %all-reduce.1 = (f32[32]{0:T(128)S(1)}, f32[32]{0:T(128)S(1)}) all-reduce(f32[32]{0:T(128)S(1)} %get-tuple-element.3, f32[32]{0:T(128)S(1)} %get-tuple-element.2), channel_id=1, replica_groups=mesh['feat'=8,'ex'=4] {'feat','ex'}, use_global_device_ids=true, to_apply=%region_3.0 | all-reduce | flops 64 | bytes 512 | tf_op jit(solution)/shard_map/psum | solution.py:36
  359.3 1.6 multiply_reduce_fusion.1
  360.9 41.1 %psum.53 = f32[32]{0:T(128)S(1)} all-reduce(f32[32]{0:T(128)S(1)} %multiply_reduce_fusion.1), channel_id=1, replica_groups=mesh['feat'=8,'ex'=4] {'feat','ex'}, use_global_device_ids=true, to_apply=%region_9.0 | all-reduce | flops 32 | bytes 256 | tf_op jit(solution)/shard_map/psum | solution.py:36
  402.0 2.3 fusion.14
  404.4 22.5 %all-gather.5.cloned.1.call-done = bf16[32,32768]{1,0:T(8,128)(2,1)} async-done(((bf16[32,8192]{1,0:T(8,128)(2,1)}), bf16[32,32768]{1,0:T(8,128)(2,1)}) %all-gather.5.cloned.1.call-update) | async-done | bytes 2097168 | tf_op jit(solution)/shard_map/all_gather | solution.py:43
  426.8 27.6 %fusion.17 = f32[32,1024]{1,0:T(8,128)} fusion(bf16[32,32768]{1,0:T(8,128)(2,1)} %all-gather.5.cloned.1.call-done, bf16[1024,32768]{1,0:T(8,128)(2,1)} %param.7), kind=kOutput, calls=%fused_computation.35 | convolution fusion | flops 2147483648 | bytes 69337088 | tf_op jit(solution)/shard_map/dot_general | solution.py:44
  454.5 70.5 %all-reduce.7.cloned.1.call-done = f32[32,1024]{1,0:T(8,128)} async-done(((f32[32,1024]{1,0:T(8,128)}), f32[32,1024]{1,0:T(8,128)}) %all-reduce.7.cloned.1.call-update) | async-done | bytes 131088 | tf_op jit(solution)/shard_map/psum | solution.py:47
  525.0 26.4 %fusion.7 = f32[32,32768]{1,0:T(8,128)} fusion(bf16[1024,32768]{1,0:T(8,128)(2,1)} %param.7, f32[32,1024]{1,0:T(8,128)} %all-reduce.7.cloned.1.call-done, f32[1024]{0:T(1024)S(1)} %get-tuple-element.6), kind=kOutput, calls=%fused_computation.19 | convolution fusion | flops 2147549184 | bytes 71438336 | tf_op jit(solution)/shard_map/dot_general | solution.py:50
  551.5 0.1 dynamic-slice_negate_fusion
  551.6 0.8 dynamic-slice_convert_fusion
  552.4 15.8 %iota_compare_fusion = pred[32768,256]{1,0:T(32,128)(4,1)} fusion(s32[32768]{0:T(1024)S(1)} %copy-done.4), kind=kLoop, calls=%fused_computation | loop fusion | flops 8388608 | bytes 8519680 | tf_op jit(solution)/shard_map/eq | solution.py:24
  568.2 27.0 %reduce-scatter.8.cloned.1.call-done = f32[32,8192]{1,0:T(8,128)} async-done(((f32[32,32768]{1,0:T(8,128)}), f32[32,8192]{1,0:T(8,128)}) %reduce-scatter.8.cloned.1.call-update) | async-done | bytes 1048592 | tf_op jit(solution)/shard_map/reduce_scatter | solution.py:49
  595.2 1.8 multiply_reduce_fusion
  597.0 39.5 %psum.55 = f32[32]{0:T(128)S(1)} all-reduce(f32[32]{0:T(128)S(1)} %multiply_reduce_fusion), channel_id=1, replica_groups=mesh['feat'=8,'ex'=4] {'feat','ex'}, use_global_device_ids=true, to_apply=%region_13.0 | all-reduce | flops 32 | bytes 256 | tf_op jit(solution)/shard_map/psum | solution.py:56
  636.5 0.4 multiply_add_fusion
  637.0 8.6 %fusion = f32[32,256]{0,1:T(8,128)S(1)} fusion(pred[32768,256]{1,0:T(32,128)(4,1)} %iota_compare_fusion, s32[]{:T(128)S(6)} %select_n.8, f32[32,8192]{1,0:T(8,128)S(1)} %multiply_add_fusion, f32[8192]{0:T(1024)S(1)} %dynamic-slice_convert_fusion), kind=kOutput, calls=%fused_computation.1 | convolution fusion | flops 805568512 | bytes 3211268 | tf_op jit(solution)/shard_map/dot_general | solution.py:63
  645.6 42.0 %all-reduce = f32[32,256]{0,1:T(8,128)S(1)} all-reduce(f32[32,256]{0,1:T(8,128)S(1)} %fusion), channel_id=5, replica_groups=mesh['feat'=8,'ex'=4] {'feat','ex'}, use_global_device_ids=true, to_apply=%region_14.0.clone | all-reduce | flops 8192 | bytes 65536
  687.6 0.7 dynamic-slice_multiply_fusion
  (34 shorter events, 0.4 us)
Async XLA Ops:
  7.2 118.0 %reduce-scatter.4.cloned.1.call-start = ((), (), s32[]{:S(2)}) async-start(), calls=%async_computation.3 | async-start | bytes 5242880 | tf_op jit(solution)/shard_map/reduce_scatter | solution.py:30
  8.1 49.8 %copy-start.5 = (s32[1024]{0:T(1024)S(1)}, s32[1024]{0:T(1024)}, u32[]{:S(2)}) copy-start(s32[1024]{0:T(1024)} %param.10) | copy-start | bytes 12292
  8.1 49.8 %copy-start.6 = (s32[1024]{0:T(1024)S(1)}, s32[1024]{0:T(1024)}, u32[]{:S(2)}) copy-start(s32[1024]{0:T(1024)} %param.9) | copy-start | bytes 12292
  8.1 49.8 %copy-start.3 = (f32[32,1024]{1,0:T(8,128)S(1)}, f32[32,1024]{1,0:T(8,128)}, u32[]{:S(2)}) copy-start(f32[32,1024]{1,0:T(8,128)} %param.11) | copy-start | bytes 393220
  83.3 66.7 %all-gather.3.cloned.1.call-start = ((), (), s32[]{:S(2)}) async-start(), calls=%async_computation.4 | async-start | bytes 2621440 | tf_op jit(solution)/shard_map/all_gather | solution.py:43
  127.2 120.9 %all-reduce.5.cloned.1.call-start = ((), (), s32[]{:S(2)}) async-start(), calls=%async_computation.5 | async-start | bytes 262144 | tf_op jit(solution)/shard_map/psum | solution.py:47
  177.6 140.8 %reduce-scatter.6.cloned.1.call-start = ((), (), s32[]{:S(2)}) async-start(), calls=%async_computation.6 | async-start | bytes 5242880 | tf_op jit(solution)/shard_map/reduce_scatter | solution.py:49
  248.2 26.5 %copy-start.4 = (s32[32768]{0:T(1024)S(1)}, s32[32768]{0:T(1024)}, u32[]{:S(2)}) copy-start(s32[32768]{0:T(1024)} %param.13) | copy-start | bytes 393220
  248.2 26.6 %copy-start.7 = (f32[256]{0:T(256)S(1)}, f32[256]{0:T(256)}, u32[]{:S(2)}) copy-start(f32[256]{0:T(256)} %param.12) | copy-start | bytes 3076
  274.6 43.8 %copy-start = (f32[32,8192]{1,0:T(8,128)S(1)}, f32[32,8192]{1,0:T(8,128)}, u32[]{:S(2)}) copy-start(f32[32,8192]{1,0:T(8,128)} %reduce-scatter.4.cloned.1.call-done) | copy-start | bytes 3145732
  274.7 152.2 %all-gather.5.cloned.1.call-start = ((), (), s32[]{:S(2)}) async-start(), calls=%async_computation.7 | async-start | bytes 2621440 | tf_op jit(solution)/shard_map/all_gather | solution.py:43
  404.3 120.7 %all-reduce.7.cloned.1.call-start = ((), (), s32[]{:S(2)}) async-start(), calls=%async_computation.8 | async-start | bytes 262144 | tf_op jit(solution)/shard_map/psum | solution.py:47
  454.5 140.7 %reduce-scatter.8.cloned.1.call-start = ((), (), s32[]{:S(2)}) async-start(), calls=%async_computation.9 | async-start | bytes 5242880 | tf_op jit(solution)/shard_map/reduce_scatter | solution.py:49
  551.5 43.7 %copy-start.1 = (f32[32,8192]{1,0:T(8,128)S(1)}, f32[32,8192]{1,0:T(8,128)}, u32[]{:S(2)}) copy-start(f32[32,8192]{1,0:T(8,128)} %reduce-scatter.6.cloned.1.call-done) | copy-start | bytes 3145732
  636.9 51.3 %copy-start.2 = (f32[32,8192]{1,0:T(8,128)}, f32[32,8192]{1,0:T(8,128)S(1)}, u32[]{:S(2)}) copy-start(f32[32,8192]{1,0:T(8,128)S(1)} %multiply_add_fusion) | copy-start | bytes 3145732
Sparse Core Ops, SparseCore 0:
  83.4 41.7 reduce-scatter.3
  127.4 22.5 all-gather.2
  177.7 70.3 all-reduce.4
  274.8 43.5 reduce-scatter.5
  404.4 22.3 all-gather.4
  454.6 70.3 all-reduce.6
  551.6 43.5 reduce-scatter.7
where the time goes:
time: 696 us; the launch traced here: 695 us
  waiting for transfers between devices  282 us (41%)
  matrix products  186 us (27%)
  blocking collectives  185 us (27%)
  other arithmetic  27.1 us (4%)
  between operations  14.3 us (2%)
    psum x2, waiting for transfers between devices, shards(): tang = lax.psum(tang, 'feat')  141 us
    psum x2, blocking collectives, norm_sum(): return lax.psum(jnp.sum(vec * vec, axis=1), ('feat', 'ex'))  80.4 us
    dot_general x2, matrix products, shards(): lax.dot_general(full_dir, examples, (((1,), (1,)), ((), ())), preferred_e...  55.3 us
    reduce_scatter x2, waiting for transfers between devices, shards(): lax.psum_scatter(jnp.dot(wtang, examples, preferred_element_type=jnp.floa...  53.6 us
    dot_general x2, matrix products, shards(): jnp.dot(wtang, examples, preferred_element_type=jnp.float32)  52.9 us
    all_gather x2, waiting for transfers between devices, shards(): lax.all_gather(direc.astype(jnp.bfloat16), 'ex', axis=1, tiled=True)  45.1 us
    unnamed x1, blocking collectives  42 us
    reduce_scatter x1, waiting for transfers between devices, shards(): rhs = lax.psum_scatter(grad_part, 'ex', scatter_dimension=1, tiled=True)  41.8 us
  transfers between devices with their start and end apart: 7, of which 7 were waited for; matrix products, arithmetic and copies ran while one was open for 5% of the time, Pallas kernels for 0%

commit v1 on v0

--- a/solution.py
+++ b/solution.py
@@ -2,6 +2,22 @@
 import jax.numpy as jnp
 from jax import lax
 from jax.sharding import PartitionSpec as P
+
+
+def collect(x, axis, dim):
+    ways, here, step = (lax.axis_size(axis), lax.axis_index(axis), x.shape[dim])
+    shape = [n * ways if d == dim else n for d, n in enumerate(x.shape)]
+    full = lax.dynamic_update_slice_in_dim(jnp.zeros(shape, x.dtype), x, here * step, axis=dim)
+    going_up = going_down = x
+    for far in range(1, ways // 2 + 1):
+        going_up = lax.ppermute(going_up, axis, [(d, (d + 1) % ways) for d in range(ways)])
+        full = lax.dynamic_update_slice_in_dim(full, going_up, (here - far) % ways * step, axis=dim)
+        if 2 * far < ways:
+            going_down = lax.ppermute(going_down, axis, [(d, (d - 1) % ways) for d in range(ways)])
+            full = lax.dynamic_update_slice_in_dim(
+                full, going_down, (here + far) % ways * step, axis=dim
+            )
+    return full
 
 
 def shards(examples, weights, labels, split, val_weight, strengths, block_ids):
@@ -40,7 +56,7 @@
     direc = rhs
     norm_now = norm_sum(resid)
     for step in range(2):
-        full_dir = lax.all_gather(direc.astype(jnp.bfloat16), "ex", axis=1, tiled=True)
+        full_dir = collect(direc.astype(jnp.bfloat16), "ex", 1)
         tang = lax.dot_general(
             full_dir, examples, (((1,), (1,)), ((), ())), preferred_element_type=jnp.float32
         )

time: 696 us -> 695 us (level)
  waiting for transfers between devices: 282 us -> 273 us
    all_gather x2 -> x0, waiting for transfers between devices: 45.1 us -> none  [shards(): lax.all_gather(direc.astype(jnp.bfloat16), 'ex', axis=1, tiled=True)]
    ppermute x0 -> x6, waiting for transfers between devices: none -> 34.8 us  [the longest x4 34.8 us: collect(): lax.ppermute(going_up, axis, [(d, (d + 1) % ways) for d in range(ways)])]
  transfers between devices with their start and end apart: 7 -> 11, of which waited for: 7 -> 9; matrix products, arithmetic and copies ran while one was open for 5% -> 5% of each run, Pallas kernels for 0% -> 0%
where the time goes in v1:
time: 695 us; the launch traced here: 694 us
  waiting for transfers between devices  273 us (39%)
  matrix products  185 us (27%)
  blocking collectives  185 us (27%)
  other arithmetic  25.2 us (4%)
  between operations  14 us (2%)
    psum x2, waiting for transfers between devices, shards(): tang = lax.psum(tang, 'feat')  143 us
    psum x2, blocking collectives, norm_sum(): return lax.psum(jnp.sum(vec * vec, axis=1), ('feat', 'ex'))  80.5 us
    dot_general x2, matrix products, shards(): lax.dot_general(full_dir, examples, (((1,), (1,)), ((), ())), preferred_e...  54.8 us
    reduce_scatter x2, waiting for transfers between devices, shards(): lax.psum_scatter(jnp.dot(wtang, examples, preferred_element_type=jnp.floa...  52.9 us
    dot_general x2, matrix products, shards(): jnp.dot(wtang, examples, preferred_element_type=jnp.float32)  52.8 us
    unnamed x1, blocking collectives  42 us
    reduce_scatter x1, waiting for transfers between devices, shards(): rhs = lax.psum_scatter(grad_part, 'ex', scatter_dimension=1, tiled=True)  41.8 us
    psum x1, blocking collectives, shards(): alpha = norm_now / lax.psum(jnp.sum(direc * image, axis=1), ('feat', 'ex'))  39.6 us
  transfers between devices with their start and end apart: 11, of which 9 were waited for; matrix products, arithmetic and copies ran while one was open for 5% of the time, Pallas kernels for 0%

profile of v1, /device:TPU:0, one launch (start us, length us, event | category | flops | bytes accessed | tf_op | source)
XLA Modules:
  0.0 694.3 jit_solution(10393611718604456008)
XLA Ops:
  8.2 26.6 %fusion.16 = f32[1,1024]{1,0:T(1,128)S(1)} fusion(bf16[1024,32768]{1,0:T(8,128)(2,1)} %param.7, bf16[32768,1]{0,1:T(2,128)(2,1)S(1)} %reshape.14), kind=kOutput, calls=%fused_computation.41 | convolution fusion | flops 67108864 | bytes 67178496 | tf_op jit(solution)/shard_map/dot_general | solution.py:33
  34.8 23.2 %psum.49 = f32[1024]{0:T(1024)S(1)} all-reduce(f32[1024]{0:T(1024)S(1)} %bitcast.13), channel_id=1, replica_groups=mesh['feat'=8,'ex'=4] {'feat'}, use_global_device_ids=true, to_apply=%region_0.0 | all-reduce | flops 1024 | bytes 8192 | tf_op jit(solution)/shard_map/psum | solution.py:33
  58.0 25.3 %fusion.5 = f32[32,32768]{1,0:T(8,128)} fusion(bf16[1024,32768]{1,0:T(8,128)(2,1)} %param.7, f32[32,1024]{1,0:T(8,128)S(1)} %copy-done.3, f32[1024]{0:T(1024)S(1)} %get-tuple-element.11), kind=kOutput, calls=%fused_computation.17 | convolution fusion | flops 2147581952 | bytes 71438336 | tf_op jit(solution)/shard_map/dot_general | solution.py:39
  83.3 41.8 %reduce-scatter.4.cloned.1.call-done = f32[32,8192]{1,0:T(8,128)} async-done(((f32[32,32768]{1,0:T(8,128)}), f32[32,8192]{1,0:T(8,128)}) %reduce-scatter.4.cloned.1.call-update) | async-done | bytes 1048592 | tf_op jit(solution)/shard_map/reduce_scatter | solution.py:46
  125.3 1.3 constant_dynamic-update-slice_fusion.7
  126.7 1.7 collective-permute-start.1
  128.4 11.8 %collective-permute-done = bf16[32,8192]{1,0:T(8,128)(2,1)S(1)} collective-permute-done((bf16[32,8192]{1,0:T(8,128)(2,1)S(1)}, bf16[32,8192]{1,0:T(8,128)(2,1)S(1)}, u32[]{:S(2)}, u32[]{:S(2)}) %collective-permute-start) | collective-permute-done | bytes 524320 | tf_op jit(solution)/shard_map/ppermute | solution.py:13
  140.3 8.5 %collective-permute-done.2 = bf16[32,8192]{1,0:T(8,128)(2,1)S(1)} collective-permute-done((bf16[32,8192]{1,0:T(8,128)(2,1)S(1)}, bf16[32,8192]{1,0:T(8,128)(2,1)S(1)}, u32[]{:S(2)}, u32[]{:S(2)}) %collective-permute-start.2) | collective-permute-done | bytes 524320 | tf_op jit(solution)/shard_map/ppermute | solution.py:13
  148.9 27.2 %fusion.17 = f32[32,1024]{1,0:T(8,128)} fusion(bf16[32,32768]{1,0:T(8,128)(2,1)S(1)} %constant_dynamic-update-slice_fusion.4, bf16[1024,32768]{1,0:T(8,128)(2,1)} %param.7), kind=kOutput, calls=%fused_computation.42 | convolution fusion | flops 2147483648 | bytes 69337088 | tf_op jit(solution)/shard_map/dot_general | solution.py:60
  176.1 70.3 %all-reduce.5.cloned.1.call-done = f32[32,1024]{1,0:T(8,128)} async-done(((f32[32,1024]{1,0:T(8,128)}), f32[32,1024]{1,0:T(8,128)}) %all-reduce.5.cloned.1.call-update) | async-done | bytes 131088 | tf_op jit(solution)/shard_map/psum | solution.py:63
  246.4 26.4 %fusion.6 = f32[32,32768]{1,0:T(8,128)} fusion(bf16[1024,32768]{1,0:T(8,128)(2,1)} %param.7, f32[32,1024]{1,0:T(8,128)} %all-reduce.5.cloned.1.call-done, f32[1024]{0:T(1024)S(1)} %get-tuple-element.10), kind=kOutput, calls=%fused_computation.18 | convolution fusion | flops 2147549184 | bytes 71438336 | tf_op jit(solution)/shard_map/dot_general | solution.py:66
  273.8 17.0 %fusion.3 = f32[1,32768]{1,0:T(1,128)S(1)} fusion(f32[256,1]{0,1:T(1,128)S(1)} %bitcast.15, s32[32768]{0:T(1024)S(1)} %copy-done.4), kind=kOutput, calls=%fused_computation.12 | convolution fusion | flops 109051904 | bytes 263168 | tf_op jit(solution)/shard_map/dot_general | solution.py:43
  290.8 25.8 %reduce-scatter.6.cloned.1.call-done = f32[32,8192]{1,0:T(8,128)} async-done(((f32[32,32768]{1,0:T(8,128)}), f32[32,8192]{1,0:T(8,128)}) %reduce-scatter.6.cloned.1.call-update) | async-done | bytes 1048592 | tf_op jit(solution)/shard_map/reduce_scatter | solution.py:65
  316.6 1.7 multiply_reduce_fusion.2
  318.3 39.5 %all-reduce.1 = (f32[32]{0:T(128)S(1)}, f32[32]{0:T(128)S(1)}) all-reduce(f32[32]{0:T(128)S(1)} %get-tuple-element.3, f32[32]{0:T(128)S(1)} %get-tuple-element.2), channel_id=1, replica_groups=mesh['feat'=8,'ex'=4] {'feat','ex'}, use_global_device_ids=true, to_apply=%region_3.0 | all-reduce | flops 64 | bytes 512 | tf_op jit(solution)/shard_map/psum | solution.py:52
  357.8 1.6 multiply_reduce_fusion.1
  359.4 41.0 %psum.53 = f32[32]{0:T(128)S(1)} all-reduce(f32[32]{0:T(128)S(1)} %multiply_reduce_fusion.1), channel_id=1, replica_groups=mesh['feat'=8,'ex'=4] {'feat','ex'}, use_global_device_ids=true, to_apply=%region_9.10 | all-reduce | flops 32 | bytes 256 | tf_op jit(solution)/shard_map/psum | solution.py:52
  400.4 1.5 broadcast.25
  401.9 1.1 constant_dynamic-update-slice_fusion.3
  403.0 1.7 collective-permute-start.4
  404.7 9.9 %collective-permute-done.3 = bf16[32,8192]{1,0:T(8,128)(2,1)S(1)} collective-permute-done((bf16[32,8192]{1,0:T(8,128)(2,1)S(1)}, bf16[32,8192]{1,0:T(8,128)(2,1)S(1)}, u32[]{:S(2)}, u32[]{:S(2)}) %collective-permute-start.3) | collective-permute-done | bytes 524320 | tf_op jit(solution)/shard_map/ppermute | solution.py:13
  414.6 2.4 collective-permute-start.5
  418.7 4.6 collective-permute-done.5
  424.1 27.6 %fusion.18 = f32[32,1024]{1,0:T(8,128)} fusion(bf16[32,32768]{1,0:T(8,128)(2,1)} %constant_dynamic-update-slice_fusion, bf16[1024,32768]{1,0:T(8,128)(2,1)} %param.7), kind=kOutput, calls=%fused_computation.43 | convolution fusion | flops 2147483648 | bytes 69337088 | tf_op jit(solution)/shard_map/dot_general | solution.py:60
  451.8 72.7 %all-reduce.7.cloned.1.call-done = f32[32,1024]{1,0:T(8,128)} async-done(((f32[32,1024]{1,0:T(8,128)}), f32[32,1024]{1,0:T(8,128)}) %all-reduce.7.cloned.1.call-update) | async-done | bytes 131088 | tf_op jit(solution)/shard_map/psum | solution.py:63
  524.5 26.4 %fusion.7 = f32[32,32768]{1,0:T(8,128)} fusion(bf16[1024,32768]{1,0:T(8,128)(2,1)} %param.7, f32[32,1024]{1,0:T(8,128)} %all-reduce.7.cloned.1.call-done, f32[1024]{0:T(1024)S(1)} %get-tuple-element.10), kind=kOutput, calls=%fused_computation.19 | convolution fusion | flops 2147549184 | bytes 71438336 | tf_op jit(solution)/shard_map/dot_general | solution.py:66
  551.7 15.8 %iota_compare_fusion = pred[32768,256]{1,0:T(32,128)(4,1)} fusion(s32[32768]{0:T(1024)S(1)} %copy-done.4), kind=kLoop, calls=%fused_computation | loop fusion | flops 8388608 | bytes 8519680 | tf_op jit(solution)/shard_map/eq | solution.py:40
  567.6 27.1 %reduce-scatter.8.cloned.1.call-done = f32[32,8192]{1,0:T(8,128)} async-done(((f32[32,32768]{1,0:T(8,128)}), f32[32,8192]{1,0:T(8,128)}) %reduce-scatter.8.cloned.1.call-update) | async-done | bytes 1048592 | tf_op jit(solution)/shard_map/reduce_scatter | solution.py:65
  594.7 1.8 multiply_reduce_fusion
  596.5 39.6 %psum.55 = f32[32]{0:T(128)S(1)} all-reduce(f32[32]{0:T(128)S(1)} %multiply_reduce_fusion), channel_id=1, replica_groups=mesh['feat'=8,'ex'=4] {'feat','ex'}, use_global_device_ids=true, to_apply=%region_13.14 | all-reduce | flops 32 | bytes 256 | tf_op jit(solution)/shard_map/psum | solution.py:72
  636.4 8.6 %fusion = f32[32,256]{0,1:T(8,128)S(1)} fusion(pred[32768,256]{1,0:T(32,128)(4,1)} %iota_compare_fusion, s32[]{:T(128)S(6)} %select_n.43, f32[32,8192]{1,0:T(8,128)S(1)} %multiply_add_fusion, f32[8192]{0:T(1024)S(1)} %dynamic-slice_convert_fusion), kind=kOutput, calls=%fused_computation.1 | convolution fusion | flops 805568512 | bytes 3211268 | tf_op jit(solution)/shard_map/dot_general | solution.py:79
  645.1 42.0 %all-reduce = f32[32,256]{0,1:T(8,128)S(1)} all-reduce(f32[32,256]{0,1:T(8,128)S(1)} %fusion), channel_id=5, replica_groups=mesh['feat'=8,'ex'=4] {'feat','ex'}, use_global_device_ids=true, to_apply=%region_14.15.clone | all-reduce | flops 8192 | bytes 65536
  (48 shorter events, 6.8 us)
Async XLA Ops:
  7.2 118.0 %reduce-scatter.4.cloned.1.call-start = ((), (), s32[]{:S(2)}) async-start(), calls=%async_computation.3 | async-start | bytes 5242880 | tf_op jit(solution)/shard_map/reduce_scatter | solution.py:46
  8.1 49.8 %copy-start.5 = (s32[1024]{0:T(1024)S(1)}, s32[1024]{0:T(1024)}, u32[]{:S(2)}) copy-start(s32[1024]{0:T(1024)} %param.10) | copy-start | bytes 12292
  8.1 49.8 %copy-start.6 = (s32[1024]{0:T(1024)S(1)}, s32[1024]{0:T(1024)}, u32[]{:S(2)}) copy-start(s32[1024]{0:T(1024)} %param.9) | copy-start | bytes 12292
  8.1 49.8 %copy-start.3 = (f32[32,1024]{1,0:T(8,128)S(1)}, f32[32,1024]{1,0:T(8,128)}, u32[]{:S(2)}) copy-start(f32[32,1024]{1,0:T(8,128)} %param.11) | copy-start | bytes 393220
  83.3 163.2 %all-reduce.5.cloned.1.call-start = ((), (), s32[]{:S(2)}) async-start(), calls=%async_computation.4 | async-start | bytes 262144 | tf_op jit(solution)/shard_map/psum | solution.py:63
  126.6 13.6 %collective-permute-start = (bf16[32,8192]{1,0:T(8,128)(2,1)S(1)}, bf16[32,8192]{1,0:T(8,128)(2,1)S(1)}, u32[]{:S(2)}, u32[]{:S(2)}) collective-permute-start(bf16[32,8192]{1,0:T(8,128)(2,1)S(1)} %get-tuple-element.9), channel_id=1, source_target_pairs={{0,1},{1,2},{2,3},{3,0},{4,5},{5,6},{6,7},{7,4},{8,9},{9,10},{10,1... | collective-permute-start | bytes 1572872 | tf_op jit(solution)/shard_map/ppermute | solution.py:13
  126.7 13.5 %collective-permute-start.1 = (bf16[32,8192]{1,0:T(8,128)(2,1)S(1)}, bf16[32,8192]{1,0:T(8,128)(2,1)S(1)}, u32[]{:S(2)}, u32[]{:S(2)}) collective-permute-start(bf16[32,8192]{1,0:T(8,128)(2,1)S(1)} %get-tuple-element.9), channel_id=1, source_target_pairs={{0,3},{1,0},{2,1},{3,2},{4,7},{5,4},{6,5},{7,6},{8,11},{9,8},{10,9... | collective-permute-start | bytes 1572872 | tf_op jit(solution)/shard_map/ppermute | solution.py:16
  140.2 8.6 %collective-permute-start.2 = (bf16[32,8192]{1,0:T(8,128)(2,1)S(1)}, bf16[32,8192]{1,0:T(8,128)(2,1)S(1)}, u32[]{:S(2)}, u32[]{:S(2)}) collective-permute-start(bf16[32,8192]{1,0:T(8,128)(2,1)S(1)} %collective-permute-done), channel_id=1, source_target_pairs={{0,1},{1,2},{2,3},{3,0},{4,5},{5,6},{6,7},{7,4},{8,9},{9,10},{10,1... | collective-permute-start | bytes 1572872 | tf_op jit(solution)/shard_map/ppermute | solution.py:13
  176.1 140.5 %reduce-scatter.6.cloned.1.call-start = ((), (), s32[]{:S(2)}) async-start(), calls=%async_computation.5 | async-start | bytes 5242880 | tf_op jit(solution)/shard_map/reduce_scatter | solution.py:65
  272.9 0.9 copy-start.4
  272.9 0.9 copy-start.7
  272.9 251.6 %all-reduce.7.cloned.1.call-start = ((), (), s32[]{:S(2)}) async-start(), calls=%async_computation.6 | async-start | bytes 262144 | tf_op jit(solution)/shard_map/psum | solution.py:63
  273.8 42.8 %copy-start = (f32[32,8192]{1,0:T(8,128)S(1)}, f32[32,8192]{1,0:T(8,128)}, u32[]{:S(2)}) copy-start(f32[32,8192]{1,0:T(8,128)} %reduce-scatter.4.cloned.1.call-done) | copy-start | bytes 3145732
  316.6 85.3 %copy-start.1 = (f32[32,8192]{1,0:T(8,128)S(1)}, f32[32,8192]{1,0:T(8,128)}, u32[]{:S(2)}) copy-start(f32[32,8192]{1,0:T(8,128)} %reduce-scatter.6.cloned.1.call-done) | copy-start | bytes 3145732
  403.0 11.7 %collective-permute-start.3 = (bf16[32,8192]{1,0:T(8,128)(2,1)S(1)}, bf16[32,8192]{1,0:T(8,128)(2,1)S(1)}, u32[]{:S(2)}, u32[]{:S(2)}) collective-permute-start(bf16[32,8192]{1,0:T(8,128)(2,1)S(1)} %get-tuple-element.7), channel_id=1, source_target_pairs={{0,1},{1,2},{2,3},{3,0},{4,5},{5,6},{6,7},{7,4},{8,9},{9,10},{10,1... | collective-permute-start | bytes 1572872 | tf_op jit(solution)/shard_map/ppermute | solution.py:13
  403.0 14.9 %collective-permute-start.4 = (bf16[32,8192]{1,0:T(8,128)(2,1)S(1)}, bf16[32,8192]{1,0:T(8,128)(2,1)S(1)}, u32[]{:S(2)}, u32[]{:S(2)}) collective-permute-start(bf16[32,8192]{1,0:T(8,128)(2,1)S(1)} %get-tuple-element.7), channel_id=1, source_target_pairs={{0,3},{1,0},{2,1},{3,2},{4,7},{5,4},{6,5},{7,6},{8,11},{9,8},{10,9... | collective-permute-start | bytes 1572872 | tf_op jit(solution)/shard_map/ppermute | solution.py:16
  414.6 8.6 %collective-permute-start.5 = (bf16[32,8192]{1,0:T(8,128)(2,1)S(1)}, bf16[32,8192]{1,0:T(8,128)(2,1)S(1)}, u32[]{:S(2)}, u32[]{:S(2)}) collective-permute-start(bf16[32,8192]{1,0:T(8,128)(2,1)S(1)} %collective-permute-done.3), channel_id=1, source_target_pairs={{0,1},{1,2},{2,3},{3,0},{4,5},{5,6},{6,7},{7,4},{8,9},{9,10},{10,1... | collective-permute-start | bytes 1572872 | tf_op jit(solution)/shard_map/ppermute | solution.py:13
  451.7 142.9 %reduce-scatter.8.cloned.1.call-start = ((), (), s32[]{:S(2)}) async-start(), calls=%async_computation.7 | async-start | bytes 5242880 | tf_op jit(solution)/shard_map/reduce_scatter | solution.py:65
  636.4 51.3 %copy-start.2 = (f32[32,8192]{1,0:T(8,128)}, f32[32,8192]{1,0:T(8,128)S(1)}, u32[]{:S(2)}) copy-start(f32[32,8192]{1,0:T(8,128)S(1)} %multiply_add_fusion) | copy-start | bytes 3145732
Sparse Core Ops, SparseCore 0:
  83.4 41.7 reduce-scatter.3
  176.2 70.1 all-reduce.4
  273.0 43.5 reduce-scatter.5
  451.8 72.6 all-reduce.6
  551.1 43.5 reduce-scatter.7
